TPU v7x, 128 devices: a whole 4x4x4 slice. The times are simulated.
128 devices in a mesh: dp: 8 (over z_hi, y), fsdp: 16 (over z_lo, x, core).
Axes of the slice: x: 4, y: 4, z: 4 (z_hi: 2, z_lo: 2; z = z_hi * 2 + z_lo), core: 2. Of those that a mesh axis runs over, the one named last changes fastest.
Arguments:
- weight: float32 [4096, 15360], P('fsdp', 'dp'), may hold values from -0.09375 to 0.09375
- history: float32 [7, 4096, 15360], P(None, 'fsdp', 'dp'), may hold values from -6 to 6
- newest: int32 [1], replicated, may hold values from 0 to 6
- band: float32 [8], replicated, may hold values from 0.5 to 1.5
- fresh: bfloat16 [4096, 15360], P('fsdp', 'dp'), may hold values from -6 to 6
- x_grad: bfloat16 [1024, 4096], P('dp', 'fsdp'), may hold values from -96 to 96
- dy_grad: bfloat16 [1024, 15360], P('dp'), may hold values from -6 to 6
- x_next: bfloat16 [6144, 4096], P('fsdp'), may hold values from -6 to 6
Outputs:
- new_weight: float32 [4096, 15360], P('fsdp', 'dp')
- noise_now: float32 [4096, 15360], P('fsdp', 'dp')
- next_out: bfloat16 [6144, 15360], P('fsdp', 'dp')
All inputs are finite; a program needn't handle non-finite values.
Results may differ from a plain program's by a relative error of at most 0.005.
Values may be sent and summed in bfloat16 or wider, within the bound.
A program may use at most 128 MiB of HBM per device.

v0:
```python
import math
import jax
import jax.numpy as jnp
from jax import lax
from jax.sharding import PartitionSpec as P

eps_value = 1e-06
learn_rate = 0.2
noise_multiplier = 0.01


def slot_weights(newest, band, slots):
    slot_index = jnp.arange(slots, dtype=jnp.int32)
    ages = (newest[0] - slot_index) % slots + 1
    table_index = jnp.arange(slots + 1, dtype=jnp.int32)
    return jnp.sum(jnp.where(ages[:, None] == table_index[None, :], band[None, :], 0.0), axis=1)


def local(weight, history, newest, band, fresh, x_grad, dy_grad, x_next):
    full_width = x_next.shape[1]
    hidden_units = dy_grad.shape[1]
    clip_bound = 2.0 * math.sqrt(full_width * hidden_units)
    dy_mine = lax.all_to_all(dy_grad, "dp", split_axis=1, concat_axis=0, tiled=True)
    x_float = x_grad.astype(jnp.float32)
    feature_sq = lax.psum(jnp.sum(x_float * x_float, axis=1), "fsdp")
    output_sq = jnp.sum(jnp.square(dy_grad.astype(jnp.float32)), axis=1)
    factor = jnp.minimum(1.0, clip_bound / jnp.sqrt(feature_sq * output_sq + eps_value))
    clipped = (factor[:, None] * x_float).astype(jnp.bfloat16)
    clipped_all = lax.all_gather(clipped, "dp", axis=0, tiled=True)
    contract = (((0,), (0,)), ((), ()))
    gradient = lax.dot_general(clipped_all, dy_mine, contract, preferred_element_type=jnp.float32)
    tokens_all = x_grad.shape[0] * lax.axis_size("dp")
    slots = history.shape[0]
    mixing = slot_weights(newest, band, slots)
    combined = jnp.tensordot(mixing, history, axes=1, precision=lax.Precision.HIGHEST)
    noise_now = (fresh.astype(jnp.float32) - combined) / band[0]
    new_weight = (
        weight - learn_rate * (gradient + noise_multiplier * clip_bound * noise_now) / tokens_all
    )
    weight_half = new_weight.astype(jnp.bfloat16)
    next_float = jnp.dot(
        x_next,
        lax.all_gather(weight_half, "fsdp", axis=0, tiled=True),
        preferred_element_type=jnp.float32,
    )
    return (new_weight, noise_now, next_float.astype(jnp.bfloat16))


def solution(mesh):
    in_specs = (
        P("fsdp", "dp"),
        P(None, "fsdp", "dp"),
        P(),
        P(),
        P("fsdp", "dp"),
        P("dp", "fsdp"),
        P("dp", None),
        P("fsdp", None),
    )
    out_specs = (P("fsdp", "dp"), P("fsdp", "dp"), P("fsdp", "dp"))
    return jax.shard_map(local, mesh=mesh, in_specs=in_specs, out_specs=out_specs, check_vma=False)
```

profile of v0, /device:TPU:1, one launch (start us, length us, event | category | flops | bytes accessed | tf_op | source)
XLA Modules:
  0.0 260.5 jit_solution(6377903200026531716)
XLA Ops:
  7.2 0.0 copy-start
  7.2 6.4 %copy.16 = bf16[128,15360]{0,1:T(8,128)(2,1)} copy(bf16[128,15360]{1,0:T(8,128)(2,1)} %param.14) | data formatting | bytes 7864320 | tf_op args[6]
  13.6 0.0 copy-start.2
  13.6 0.0 copy-start.3
  13.6 8.5 %all-to-all-start = ((bf16[128,8,1920]{0,2,1:T(8,128)(2,1)}), bf16[128,8,1920]{0,2,1:T(8,128)(2,1)}, u32[]{:S(2)}, u32[]{:S(2)}) async-start(bf16[128,8,1920]{0,2,1:T(8,128)(2,1)} %bitcast.20), calls=%async_computation | async-start | bytes 7864320 | tf_op jit(solution)/shard_map/all_to_all | solution.py:23
  22.0 0.0 all-gather.2.cloned.1.call-start
  22.7 0.0 copy-done.2
  22.7 0.1 fusion.6
  22.9 33.2 %psum.7 = f32[128]{0:T(128)S(1)} all-reduce(f32[128]{0:T(128)S(1)} %fusion.6), channel_id=1, replica_groups=mesh['dp'=8,'fsdp'=16] {'fsdp'}, use_global_device_ids=true, to_apply=%region_1.0 | all-reduce | flops 128 | bytes 1024 | tf_op jit(solution)/shard_map/psum | solution.py:25
  56.1 0.0 copy-done.3
  56.1 0.2 select_reduce_fusion
  56.3 3.0 %multiply_reduce_fusion = f32[128]{0:T(128)S(1)} fusion(bf16[128,15360]{1,0:T(8,128)(2,1)} %param.14), kind=kLoop, calls=%fused_computation.2 | loop fusion | flops 5898112 | bytes 3932672 | tf_op jit(solution)/shard_map/reduce_sum | solution.py:26
  59.3 0.1 fusion.7
  59.4 44.9 %all_gather.6 = bf16[1024,256]{1,0:T(8,128)(2,1)} all-gather(bf16[128,256]{1,0:T(8,128)(2,1)S(1)} %fusion.7), channel_id=1, replica_groups=mesh['dp'=8,'fsdp'=16] {'dp'}, dimensions={0}, use_global_device_ids=true | all-gather | bytes 589824 | tf_op jit(solution)/shard_map/all_gather | solution.py:29
  104.2 0.0 copy-start.1
  104.2 26.8 %fusion = f32[1,256,1920]{2,0,1:T(1,128)S(1)} fusion(f32[7,256,1920]{2,1,0:T(8,128)} %param.9, f32[7]{0:T(128)S(1)} %select_reduce_fusion), kind=kOutput, calls=%fused_computation | convolution fusion | flops 41287680 | bytes 15728668 | tf_op jit(solution)/shard_map/dot_general | solution.py:35
  131.1 0.0 copy-done.1
  131.1 1.5 fusion.5
  132.6 0.0 all-to-all-done
  132.6 6.4 %copy.17 = bf16[8,128,1920]{2,1,0:T(8,128)(2,1)} copy(bf16[8,128,1920]{1,2,0:T(8,128)(2,1)} %bitcast.1) | data formatting | bytes 7864320 | tf_op jit(solution)/shard_map/all_to_all | solution.py:23
  139.0 6.4 %fusion.10 = (bf16[256,1920]{1,0:T(8,128)(2,1)}, f32[256,1920]{1,0:T(8,128)}) fusion(f32[256,1920]{1,0:T(8,128)} %param.8, f32[256,1920]{1,0:T(8,128)} %fusion.5, bf16[1024,256]{1,0:T(8,128)(2,1)} %all_gather.6, bf16[1024,1920]{1,0:T(8,128)(2,1)} %bitcast.21), kind=kOutput, calls=%fused_computation.20 | convolution fusion | flops 1009090560 | bytes 11337728 | tf_op jit(solution)/shard_map/dot_general | solution.py:31
  145.4 0.0 all-gather.2.cloned.1.call-update
  145.4 92.6 %all-gather.2.cloned.1.call-done = bf16[4096,1920]{1,0:T(8,128)(2,1)} async-done(((bf16[256,1920]{1,0:T(8,128)(2,1)}), bf16[4096,1920]{1,0:T(8,128)(2,1)}) %all-gather.2.cloned.1.call-update) | async-done | bytes 15728656 | tf_op jit(solution)/shard_map/all_gather | solution.py:43
  238.0 0.0 copy-done
  238.0 13.1 %fusion.4 = bf16[384,1920]{0,1:T(8,128)(2,1)} fusion(bf16[4096,1920]{1,0:T(8,128)(2,1)} %all-gather.2.cloned.1.call-done, bf16[384,4096]{1,0:T(8,128)(2,1)S(1)} %copy-done), kind=kOutput, calls=%fused_computation.7 | convolution fusion | flops 6040535040 | bytes 20348928 | tf_op jit(solution)/shard_map/dot_general | solution.py:41
  251.1 2.5 copy.18
  (2 shorter events, 0.0 us)
Async XLA Ops:
  7.2 230.8 %copy-start = (bf16[384,4096]{1,0:T(8,128)(2,1)S(1)}, bf16[384,4096]{1,0:T(8,128)(2,1)}, u32[]{:S(2)}) copy-start(bf16[384,4096]{1,0:T(8,128)(2,1)} %param.15) | copy-start | bytes 9437188
  13.6 9.2 %copy-start.2 = (bf16[128,256]{1,0:T(8,128)(2,1)S(1)}, bf16[128,256]{1,0:T(8,128)(2,1)}, u32[]{:S(2)}) copy-start(bf16[128,256]{1,0:T(8,128)(2,1)} %param.13) | copy-start | bytes 196612
  13.6 42.5 %copy-start.3 = (f32[8]{0:T(128)S(1)}, f32[8]{0:T(128)}, u32[]{:S(2)}) copy-start(f32[8]{0:T(128)} %param.11) | copy-start | bytes 100
  13.6 119.0 %all-to-all-start = ((bf16[128,8,1920]{0,2,1:T(8,128)(2,1)}), bf16[128,8,1920]{0,2,1:T(8,128)(2,1)}, u32[]{:S(2)}, u32[]{:S(2)}) async-start(bf16[128,8,1920]{0,2,1:T(8,128)(2,1)} %bitcast.20), calls=%async_computation | async-start | bytes 7864320 | tf_op jit(solution)/shard_map/all_to_all | solution.py:23
  22.0 215.9 %all-gather.2.cloned.1.call-start = ((), (), s32[]{:S(2)}) async-start(), calls=%async_computation.1 | async-start | bytes 16711680 | tf_op jit(solution)/shard_map/all_gather | solution.py:43
  104.2 26.8 %copy-start.1 = (bf16[256,1920]{1,0:T(8,128)(2,1)S(1)}, bf16[256,1920]{1,0:T(8,128)(2,1)}, u32[]{:S(2)}) copy-start(bf16[256,1920]{1,0:T(8,128)(2,1)} %param.12) | copy-start | bytes 2949124
Sparse Core Ops, SparseCore 0:
  145.5 92.3 all-gather.1
where the time goes:
time: 261 us; the launch traced here: 260 us
  waiting for transfers between devices  92.6 us (35%)
  blocking collectives  78.1 us (30%)
  matrix products  46.4 us (18%)
  local copies, waits for them, and re-layouts  15.4 us (6%)
  between operations  14.7 us (6%)
  starting transfers between devices  8.49 us (3%)
  other arithmetic  4.86 us (2%)
    all_gather x1, waiting for transfers between devices, local(): lax.all_gather(weight_half, 'fsdp', axis=0, tiled=True)  92.6 us
    all_gather x1, blocking collectives, local(): clipped_all = lax.all_gather(clipped, 'dp', axis=0, tiled=True)  44.9 us
    psum x1, blocking collectives, local(): feature_sq = lax.psum(jnp.sum(x_float * x_float, axis=1), 'fsdp')  33.2 us
    dot_general x1, matrix products, local(): jnp.tensordot(mixing, history, axes=1, precision=lax.Precision.HIGHEST)  26.8 us
    dot_general x1, matrix products, local(): jnp.dot(x_next, lax.all_gather(weight_half, 'fsdp', axis=0, tiled=True),...  13.1 us
    unnamed x10, local copies, waits for them, and re-layouts  8.98 us
    all_to_all x1, starting transfers between devices, local(): lax.all_to_all(dy_grad, 'dp', split_axis=1, concat_axis=0, tiled=True)  8.45 us
    dot_general x1, matrix products, local(): lax.dot_general(clipped_all, dy_mine, contract, preferred_element_type=jn...  6.44 us
  transfers between devices with their start and end apart: 2, of which 1 were waited for; matrix products, arithmetic and copies ran while one was open for 12% of the time, Pallas kernels for 0%

commit v1 on v0

--- a/solution.py
+++ b/solution.py
@@ -3,6 +3,7 @@
 import jax.numpy as jnp
 from jax import lax
 from jax.sharding import PartitionSpec as P
+from jax.lax import all_to_all, axis_size
 
 eps_value = 1e-06
 learn_rate = 0.2
@@ -38,10 +39,11 @@
         weight - learn_rate * (gradient + noise_multiplier * clip_bound * noise_now) / tokens_all
     )
     weight_half = new_weight.astype(jnp.bfloat16)
+    cut_widths_over_axis = lambda arr_in: jnp.concatenate(
+        all_to_all(jnp.stack([arr_in for _ in range(axis_size("fsdp"))]), "fsdp", 0, 0), axis=0
+    )
     next_float = jnp.dot(
-        x_next,
-        lax.all_gather(weight_half, "fsdp", axis=0, tiled=True),
-        preferred_element_type=jnp.float32,
+        x_next, cut_widths_over_axis(weight_half), preferred_element_type=jnp.float32
     )
     return (new_weight, noise_now, next_float.astype(jnp.bfloat16))
 

time: 261 us -> 337 us (1.29)
  blocking collectives: 78.1 us -> 261 us
  waiting for transfers between devices: 92.6 us -> 0.01 us
  between operations: 14.7 us -> 1.35 us
  matrix products: 46.4 us -> 42.7 us
    all_to_all x0 -> x1, blocking collectives: none -> 183 us  [local(): all_to_all(jnp.stack([arr_in for _ in range(axis_size('fsdp'))]), 'fsdp',...]
    all_gather x1 -> x0, waiting for transfers between devices: 92.6 us -> none  [local(): lax.all_gather(weight_half, 'fsdp', axis=0, tiled=True)]
    dot_general x1, matrix products: 13.1 us -> 9.72 us  [local(): jnp.dot(x_next, cut_widths_over_axis(weight_half), preferred_element_type...]
  transfers between devices with their start and end apart: 2 -> 1, of which waited for: 1 -> 0; matrix products, arithmetic and copies ran while one was open for 12% -> 9% of each run, Pallas kernels for 0% -> 0%
where the time goes in v1:
time: 337 us; the launch traced here: 336 us
  blocking collectives  261 us (77%)
  matrix products  42.7 us (13%)
  local copies, waits for them, and re-layouts  17.4 us (5%)
  starting transfers between devices  8.45 us (3%)
  other arithmetic  4.86 us (1%)
    all_to_all x1, blocking collectives, local(): all_to_all(jnp.stack([arr_in for _ in range(axis_size('fsdp'))]), 'fsdp',...  183 us
    all_gather x1, blocking collectives, local(): clipped_all = lax.all_gather(clipped, 'dp', axis=0, tiled=True)  44.9 us
    psum x1, blocking collectives, local(): feature_sq = lax.psum(jnp.sum(x_float * x_float, axis=1), 'fsdp')  33.2 us
    dot_general x1, matrix products, local(): jnp.tensordot(mixing, history, axes=1, precision=lax.Precision.HIGHEST)  26.8 us
    dot_general x1, matrix products, local(): jnp.dot(x_next, cut_widths_over_axis(weight_half), preferred_element_type...  9.72 us
    unnamed x10, local copies, waits for them, and re-layouts  8.98 us
    all_to_all x1, starting transfers between devices, local(): lax.all_to_all(dy_grad, 'dp', split_axis=1, concat_axis=0, tiled=True)  8.45 us
  transfers between devices with their start and end apart: 1, of which 0 were waited for; matrix products, arithmetic and copies ran while one was open for 9% of the time, Pallas kernels for 0%

profile of v1, /device:TPU:1, one launch (start us, length us, event | category | flops | bytes accessed | tf_op | source)
XLA Modules:
  0.0 336.2 jit_solution(1325512233760579883)
XLA Ops:
  0.6 0.0 copy-start
  0.6 6.4 %copy.16 = bf16[128,15360]{0,1:T(8,128)(2,1)} copy(bf16[128,15360]{1,0:T(8,128)(2,1)} %param.14) | data formatting | bytes 7864320 | tf_op args[6]
  7.1 0.0 copy-start.2
  7.1 0.0 copy-start.3
  7.1 8.5 %all-to-all-start = ((bf16[128,8,1920]{0,2,1:T(8,128)(2,1)}), bf16[128,8,1920]{0,2,1:T(8,128)(2,1)}, u32[]{:S(2)}, u32[]{:S(2)}) async-start(bf16[128,8,1920]{0,2,1:T(8,128)(2,1)} %bitcast.22), calls=%async_computation | async-start | bytes 7864320 | tf_op jit(solution)/shard_map/all_to_all | solution.py:24
  16.2 0.0 copy-done.2
  16.2 0.1 fusion.6
  16.3 33.2 %psum.7 = f32[128]{0:T(128)S(1)} all-reduce(f32[128]{0:T(128)S(1)} %fusion.6), channel_id=1, replica_groups=mesh['dp'=8,'fsdp'=16] {'fsdp'}, use_global_device_ids=true, to_apply=%region_1.0 | all-reduce | flops 128 | bytes 1024 | tf_op jit(solution)/shard_map/psum | solution.py:26
  49.5 0.0 copy-done.3
  49.6 0.2 select_reduce_fusion
  49.7 3.0 multiply_reduce_fusion
  52.7 0.1 fusion.7
  52.8 44.9 %all_gather.3 = bf16[1024,256]{1,0:T(8,128)(2,1)} all-gather(bf16[128,256]{1,0:T(8,128)(2,1)S(1)} %fusion.7), channel_id=1, replica_groups=mesh['dp'=8,'fsdp'=16] {'dp'}, dimensions={0}, use_global_device_ids=true | all-gather | bytes 589824 | tf_op jit(solution)/shard_map/all_gather | solution.py:30
  97.7 0.0 copy-start.1
  97.7 26.8 %fusion = f32[1,256,1920]{2,0,1:T(1,128)S(1)} fusion(f32[7,256,1920]{2,1,0:T(8,128)} %param.9, f32[7]{0:T(128)S(1)} %select_reduce_fusion), kind=kOutput, calls=%fused_computation | convolution fusion | flops 41287680 | bytes 15728668 | tf_op jit(solution)/shard_map/dot_general | solution.py:36
  124.5 0.0 copy-done.1
  124.5 1.5 fusion.5
  126.0 0.0 all-to-all-done
  126.0 6.4 %copy.17 = bf16[8,128,1920]{2,1,0:T(8,128)(2,1)} copy(bf16[8,128,1920]{1,2,0:T(8,128)(2,1)} %bitcast.1) | data formatting | bytes 7864320 | tf_op jit(solution)/shard_map/all_to_all | solution.py:24
  132.4 6.1 %fusion.10 = (bf16[256,1920]{1,0:T(8,128)(2,1)S(1)}, f32[256,1920]{1,0:T(8,128)}) fusion(f32[256,1920]{1,0:T(8,128)} %param.8, f32[256,1920]{1,0:T(8,128)} %fusion.5, bf16[1024,256]{1,0:T(8,128)(2,1)} %all_gather.3, bf16[1024,1920]{1,0:T(8,128)(2,1)} %bitcast.23), kind=kOutput, calls=%fused_computation.20 | convolution fusion | flops 1009090560 | bytes 11337728 | tf_op jit(solution)/shard_map/dot_general | solution.py:32
  138.5 2.0 stack.2
  140.6 183.3 %all_to_all.24 = bf16[16,256,1920]{2,1,0:T(8,128)(2,1)S(1)} all-to-all(bf16[16,256,1920]{2,1,0:T(8,128)(2,1)S(1)} %stack.2), channel_id=1, replica_groups=mesh['dp'=8,'fsdp'=16] {'fsdp'}, dimensions={0} | all-to-all | bytes 31457280 | tf_op jit(solution)/shard_map/all_to_all | solution.py:43
  323.9 0.0 copy-done
  323.9 9.7 %fusion.4 = bf16[384,1920]{0,1:T(8,128)(2,1)} fusion(bf16[4096,1920]{1,0:T(8,128)(2,1)S(1)} %bitcast.21, bf16[384,4096]{1,0:T(8,128)(2,1)S(1)} %copy-done), kind=kOutput, calls=%fused_computation.7 | convolution fusion | flops 6040535040 | bytes 20348928 | tf_op jit(solution)/shard_map/dot_general | solution.py:45
  333.6 2.5 copy.18
  (2 shorter events, 0.0 us)
Async XLA Ops:
  0.6 323.2 %copy-start = (bf16[384,4096]{1,0:T(8,128)(2,1)S(1)}, bf16[384,4096]{1,0:T(8,128)(2,1)}, u32[]{:S(2)}) copy-start(bf16[384,4096]{1,0:T(8,128)(2,1)} %param.15) | copy-start | bytes 9437188
  7.1 9.1 %copy-start.2 = (bf16[128,256]{1,0:T(8,128)(2,1)S(1)}, bf16[128,256]{1,0:T(8,128)(2,1)}, u32[]{:S(2)}) copy-start(bf16[128,256]{1,0:T(8,128)(2,1)} %param.13) | copy-start | bytes 196612
  7.1 42.5 %copy-start.3 = (f32[8]{0:T(128)S(1)}, f32[8]{0:T(128)}, u32[]{:S(2)}) copy-start(f32[8]{0:T(128)} %param.11) | copy-start | bytes 100
  7.1 119.0 %all-to-all-start = ((bf16[128,8,1920]{0,2,1:T(8,128)(2,1)}), bf16[128,8,1920]{0,2,1:T(8,128)(2,1)}, u32[]{:S(2)}, u32[]{:S(2)}) async-start(bf16[128,8,1920]{0,2,1:T(8,128)(2,1)} %bitcast.22), calls=%async_computation | async-start | bytes 7864320 | tf_op jit(solution)/shard_map/all_to_all | solution.py:24
  97.7 26.8 %copy-start.1 = (bf16[256,1920]{1,0:T(8,128)(2,1)S(1)}, bf16[256,1920]{1,0:T(8,128)(2,1)}, u32[]{:S(2)}) copy-start(bf16[256,1920]{1,0:T(8,128)(2,1)} %param.12) | copy-start | bytes 2949124

commit v2 on v0

--- a/solution.py
+++ b/solution.py
@@ -22,7 +22,8 @@
     clip_bound = 2.0 * math.sqrt(full_width * hidden_units)
     dy_mine = lax.all_to_all(dy_grad, "dp", split_axis=1, concat_axis=0, tiled=True)
     x_float = x_grad.astype(jnp.float32)
-    feature_sq = lax.psum(jnp.sum(x_float * x_float, axis=1), "fsdp")
+    block_here = jnp.sum(x_float * x_float, axis=1)
+    feature_sq = jnp.sum(lax.all_gather(block_here, axis_name="fsdp"), axis=0)
     output_sq = jnp.sum(jnp.square(dy_grad.astype(jnp.float32)), axis=1)
     factor = jnp.minimum(1.0, clip_bound / jnp.sqrt(feature_sq * output_sq + eps_value))
     clipped = (factor[:, None] * x_float).astype(jnp.bfloat16)

time: 261 us -> 260 us (level)
    psum x1 -> x0, blocking collectives: 33.2 us -> none  [local(): feature_sq = lax.psum(jnp.sum(x_float * x_float, axis=1), 'fsdp')]
    all_gather x0 -> x1, blocking collectives: none -> 21.7 us  [local(): feature_sq = jnp.sum(lax.all_gather(block_here, axis_name='fsdp'), axis=0)]
    all_gather x1, blocking collectives: 44.9 us -> 55.7 us  [local(): clipped_all = lax.all_gather(clipped, 'dp', axis=0, tiled=True)]
where the time goes in v2:
time: 260 us
  waiting for transfers between devices  92.2 us (35%)
  blocking collectives  77.4 us (30%)
  matrix products  46.4 us (18%)
  local copies, waits for them, and re-layouts  15.4 us (6%)
  between operations  14.7 us (6%)
  starting transfers between devices  8.49 us (3%)
  other arithmetic  4.9 us (2%)
    all_gather x1, waiting for transfers between devices, local(): lax.all_gather(weight_half, 'fsdp', axis=0, tiled=True)  92.2 us
    all_gather x1, blocking collectives, local(): clipped_all = lax.all_gather(clipped, 'dp', axis=0, tiled=True)  55.7 us
    dot_general x1, matrix products, local(): jnp.tensordot(mixing, history, axes=1, precision=lax.Precision.HIGHEST)  26.8 us
    all_gather x1, blocking collectives, local(): feature_sq = jnp.sum(lax.all_gather(block_here, axis_name='fsdp'), axis=0)  21.7 us
    dot_general x1, matrix products, local(): jnp.dot(x_next, lax.all_gather(weight_half, 'fsdp', axis=0, tiled=True),...  13.1 us
    unnamed x10, local copies, waits for them, and re-layouts  8.98 us
    all_to_all x1, starting transfers between devices, local(): lax.all_to_all(dy_grad, 'dp', split_axis=1, concat_axis=0, tiled=True)  8.45 us
    dot_general x1, matrix products, local(): lax.dot_general(clipped_all, dy_mine, contract, preferred_element_type=jn...  6.44 us
  transfers between devices with their start and end apart: 2, of which 1 were waited for; matrix products, arithmetic and copies ran while one was open for 12% of the time, Pallas kernels for 0%

profile of v2, /device:TPU:1, one launch (start us, length us, event | category | flops | bytes accessed | tf_op | source)
XLA Modules:
  0.0 259.5 jit_solution(17001466251793879837)
XLA Ops:
  7.2 0.0 copy-start
  7.2 6.4 %copy.19 = bf16[128,15360]{0,1:T(8,128)(2,1)} copy(bf16[128,15360]{1,0:T(8,128)(2,1)} %param.14) | data formatting | bytes 7864320 | tf_op args[6]
  13.6 0.0 copy-start.2
  13.6 0.0 copy-start.3
  13.6 8.5 %all-to-all-start = ((bf16[128,8,1920]{0,2,1:T(8,128)(2,1)}), bf16[128,8,1920]{0,2,1:T(8,128)(2,1)}, u32[]{:S(2)}, u32[]{:S(2)}) async-start(bf16[128,8,1920]{0,2,1:T(8,128)(2,1)} %bitcast.21), calls=%async_computation | async-start | bytes 7864320 | tf_op jit(solution)/shard_map/all_to_all | solution.py:23
  22.0 0.0 all-gather.4.cloned.1.call-start
  22.7 0.0 copy-done.2
  22.7 0.1 fusion.6
  22.9 21.7 %all-gather.1 = f32[16,1,128]{2,1,0:T(1,128)S(1)} all-gather(f32[1,1,128]{2,1,0:T(1,128)S(1)} %bitcast.23), channel_id=2, replica_groups=mesh['dp'=8,'fsdp'=16] {'fsdp'}, dimensions={0}, use_global_device_ids=true | all-gather | bytes 8704 | tf_op jit(solution)/shard_map/all_gather | solution.py:26
  44.6 0.0 copy-done.3
  44.6 0.2 select_reduce_fusion
  44.8 3.0 %multiply_reduce_fusion = f32[128]{0:T(128)S(1)} fusion(bf16[128,15360]{1,0:T(8,128)(2,1)} %param.14), kind=kLoop, calls=%fused_computation.2 | loop fusion | flops 5898112 | bytes 3932672 | tf_op jit(solution)/shard_map/reduce_sum | solution.py:27
  47.7 0.1 fusion.7
  47.9 55.7 %all_gather.14 = bf16[1024,256]{1,0:T(8,128)(2,1)} all-gather(bf16[128,256]{1,0:T(8,128)(2,1)S(1)} %fusion.7), channel_id=1, replica_groups=mesh['dp'=8,'fsdp'=16] {'dp'}, dimensions={0}, use_global_device_ids=true | all-gather | bytes 589824 | tf_op jit(solution)/shard_map/all_gather | solution.py:30
  103.6 0.0 copy-start.1
  103.6 26.8 %fusion = f32[1,256,1920]{2,0,1:T(1,128)S(1)} fusion(f32[7,256,1920]{2,1,0:T(8,128)} %param.9, f32[7]{0:T(128)S(1)} %select_reduce_fusion), kind=kOutput, calls=%fused_computation | convolution fusion | flops 41287680 | bytes 15728668 | tf_op jit(solution)/shard_map/dot_general | solution.py:36
  130.4 0.0 copy-done.1
  130.5 1.5 fusion.5
  132.0 0.0 all-to-all-done
  132.0 6.4 %copy.20 = bf16[8,128,1920]{2,1,0:T(8,128)(2,1)} copy(bf16[8,128,1920]{1,2,0:T(8,128)(2,1)} %bitcast.2) | data formatting | bytes 7864320 | tf_op jit(solution)/shard_map/all_to_all | solution.py:23
  138.3 6.4 %fusion.10 = (bf16[256,1920]{1,0:T(8,128)(2,1)}, f32[256,1920]{1,0:T(8,128)}) fusion(f32[256,1920]{1,0:T(8,128)} %param.8, f32[256,1920]{1,0:T(8,128)} %fusion.5, bf16[1024,256]{1,0:T(8,128)(2,1)} %all_gather.14, bf16[1024,1920]{1,0:T(8,128)(2,1)} %bitcast.22), kind=kOutput, calls=%fused_computation.20 | convolution fusion | flops 1009090560 | bytes 11337728 | tf_op jit(solution)/shard_map/dot_general | solution.py:32
  144.8 0.0 all-gather.4.cloned.1.call-update
  144.8 92.2 %all-gather.4.cloned.1.call-done = bf16[4096,1920]{1,0:T(8,128)(2,1)} async-done(((bf16[256,1920]{1,0:T(8,128)(2,1)}), bf16[4096,1920]{1,0:T(8,128)(2,1)}) %all-gather.4.cloned.1.call-update) | async-done | bytes 15728656 | tf_op jit(solution)/shard_map/all_gather | solution.py:44
  237.0 0.0 copy-done
  237.0 13.1 %fusion.4 = bf16[384,1920]{0,1:T(8,128)(2,1)} fusion(bf16[4096,1920]{1,0:T(8,128)(2,1)} %all-gather.4.cloned.1.call-done, bf16[384,4096]{1,0:T(8,128)(2,1)S(1)} %copy-done), kind=kOutput, calls=%fused_computation.7 | convolution fusion | flops 6040535040 | bytes 20348928 | tf_op jit(solution)/shard_map/dot_general | solution.py:42
  250.1 2.5 copy.21
  (3 shorter events, 0.1 us)
Async XLA Ops:
  7.2 229.9 %copy-start = (bf16[384,4096]{1,0:T(8,128)(2,1)S(1)}, bf16[384,4096]{1,0:T(8,128)(2,1)}, u32[]{:S(2)}) copy-start(bf16[384,4096]{1,0:T(8,128)(2,1)} %param.15) | copy-start | bytes 9437188
  13.6 9.2 %copy-start.2 = (bf16[128,256]{1,0:T(8,128)(2,1)S(1)}, bf16[128,256]{1,0:T(8,128)(2,1)}, u32[]{:S(2)}) copy-start(bf16[128,256]{1,0:T(8,128)(2,1)} %param.13) | copy-start | bytes 196612
  13.6 31.0 %copy-start.3 = (f32[8]{0:T(128)S(1)}, f32[8]{0:T(128)}, u32[]{:S(2)}) copy-start(f32[8]{0:T(128)} %param.11) | copy-start | bytes 100
  13.6 118.4 %all-to-all-start = ((bf16[128,8,1920]{0,2,1:T(8,128)(2,1)}), bf16[128,8,1920]{0,2,1:T(8,128)(2,1)}, u32[]{:S(2)}, u32[]{:S(2)}) async-start(bf16[128,8,1920]{0,2,1:T(8,128)(2,1)} %bitcast.21), calls=%async_computation | async-start | bytes 7864320 | tf_op jit(solution)/shard_map/all_to_all | solution.py:23
  22.0 215.0 %all-gather.4.cloned.1.call-start = ((), (), s32[]{:S(2)}) async-start(), calls=%async_computation.1 | async-start | bytes 16711680 | tf_op jit(solution)/shard_map/all_gather | solution.py:44
  103.6 26.9 %copy-start.1 = (bf16[256,1920]{1,0:T(8,128)(2,1)S(1)}, bf16[256,1920]{1,0:T(8,128)(2,1)}, u32[]{:S(2)}) copy-start(bf16[256,1920]{1,0:T(8,128)(2,1)} %param.12) | copy-start | bytes 2949124
Sparse Core Ops, SparseCore 0:
  144.9 92.0 all-gather.3
